TPU v7x, 32 devices: a whole 2x2x4 slice. The times are simulated.
32 devices in a mesh: lat: 4 (over y, x), lon: 8 (over z, core).
Axes of the slice: x: 2, y: 2, z: 4, core: 2. Of those that a mesh axis runs over, the one named last changes fastest.
Arguments:
- predicted_quantities: bfloat16 [3, 8, 256, 4096], P(None, None, 'lat', 'lon'), may hold values from -60 to 60
- monitor_coefficients: float32 [8], replicated, may hold values from 0.2 to 2
- departing_pieces: int32 [4, 8, 8, 32], P('lat', 'lon'), may hold values from 0 to 255
- departing_occupancy: int32 [4, 8, 8], P('lat', 'lon'), may hold values from 1 to 32, as said below
- arriving_pieces: int32 [4, 8, 8, 32], P('lat', 'lon'), may hold values from 0 to 255
- interpolant_coefficients: bfloat16 [4, 8, 8, 32, 128, 128], P('lat', 'lon'), may hold values from -0.5 to 0.5
Outputs:
- potential: float32 [256, 4096], P('lat', 'lon')
- scaled_residual: float32 [256, 4096], P('lat', 'lon')
Inputs may be any that keep to these rules, and one draw needn't show every extreme that they name: `departing_occupancy`: in each lat row a quarter of the lon indices, drawn from the seed, receive 32 tiles from every device of the row; every other count is at most 16.
All inputs are finite; a program needn't handle non-finite values.
Results may differ from a plain program's by a relative error of at most 0.00087.
Values may be sent and summed in bfloat16 or wider, within the bound.
No kernel may reach another device: no remote copies, remote signals or barrier semaphores. Data moves between devices by JAX's collectives and lax.ppermute only.
A program may use at most 64 MiB of HBM per device.

v0:
```python
import jax
import jax.numpy as jnp
from jax import lax
from jax.sharding import PartitionSpec as P

FIELDS = 8
TILE = 128
CAP = 32
SWEEPS = 3
TILES = 256


def extended(array, sides, width, wrap):
    for axis, dim in sides:
        count, length = (lax.axis_size(axis), array.shape[dim])
        up = [(i, (i + 1) % count) for i in range(count if wrap else count - 1)]
        down = [(j, i) for i, j in up]
        last = lax.slice_in_dim(array, length - width, length, axis=dim)
        initial = lax.slice_in_dim(array, 0, width, axis=dim)
        before = lax.ppermute(last, axis, up)
        after = lax.ppermute(initial, axis, down)
        array = jnp.concatenate([before, array, after], axis=dim)
    return array


def derivatives(potential):
    widened = extended(potential, (("lon", 1),), 1, True)
    padded = extended(widened, (("lat", 0),), 1, False)
    centre = padded[1:-1, 1:-1]
    east = padded[1:-1, 2:]
    west = padded[1:-1, :-2]
    north = padded[2:, 1:-1]
    south = padded[:-2, 1:-1]
    mixed = (padded[2:, 2:] - padded[2:, :-2] - padded[:-2, 2:] + padded[:-2, :-2]) * 0.25
    zonal_derivative = (east - west) * 0.5
    meridional_derivative = (north - south) * 0.5
    second_lon = east - 2.0 * centre + west
    second_lat = north - 2.0 * centre + south
    determinant = (1.0 + second_lon) * (1.0 + second_lat) - mixed * mixed
    return (zonal_derivative, meridional_derivative, determinant)


def per_device(
    predicted_quantities,
    monitor_coefficients,
    departing_pieces,
    departing_occupancy,
    arriving_pieces,
    interpolant_coefficients,
):
    horizontal_accumulated = predicted_quantities.shape[2]
    vertical_accumulated = predicted_quantities.shape[3]
    lon_count = lax.axis_size("lon")
    cell_total = horizontal_accumulated * vertical_accumulated * lax.axis_size("lat") * lon_count
    tile_ids = departing_pieces[0, 0]
    slot_counts = departing_occupancy[0, 0]
    target_ids = arriving_pieces[0, 0].reshape(-1)
    blocks = interpolant_coefficients[0, 0]
    slot_range = jnp.arange(CAP, dtype=jnp.int32)[None, :]
    flat_ids = tile_ids.reshape(-1)
    live_slots = slot_range < slot_counts[:, None]
    potential = jnp.zeros((horizontal_accumulated, vertical_accumulated), jnp.float32)
    scaled = jnp.zeros((horizontal_accumulated, vertical_accumulated), jnp.float32)
    for sweep_index in range(SWEEPS):
        zonal_derivative, meridional_derivative, determinant = derivatives(potential)
        displaced_nodes = (
            predicted_quantities[0]
            + zonal_derivative[None] * predicted_quantities[1]
            + meridional_derivative[None] * predicted_quantities[2]
        )
        sent = displaced_nodes.astype(jnp.bfloat16)
        tile_data = sent.reshape(FIELDS, TILES, TILE)
        picked = jnp.take(tile_data, flat_ids, axis=1)
        picked = picked.reshape(FIELDS, lon_count, CAP, TILE)
        picked = jnp.where(live_slots[None, :, :, None], picked, jnp.zeros((), jnp.bfloat16))
        picked = lax.all_to_all(picked, "lon", split_axis=1, concat_axis=1, tiled=True)
        contrib = jnp.einsum("fskp,skpq->skfq", picked, blocks, preferred_element_type=jnp.float32)
        contrib = contrib.reshape(lon_count * CAP, FIELDS, TILE)
        summed = jax.ops.segment_sum(contrib, target_ids, num_segments=TILES)
        interp = summed.transpose(1, 0, 2).reshape(
            FIELDS, horizontal_accumulated, vertical_accumulated
        )
        blended = displaced_nodes + interp
        monitor = jnp.sqrt(
            1.0 + jnp.sum(monitor_coefficients[:, None, None] * blended * blended, axis=0)
        )
        balance = monitor * determinant
        target = lax.psum(jnp.sum(balance), ("lat", "lon")) / cell_total
        residual = balance - target
        variance = lax.psum(jnp.sum(residual * residual), ("lat", "lon")) / cell_total
        spread = jnp.sqrt(variance + 1e-06)
        potential = potential + 0.5 * residual / (monitor * spread)
        scaled = residual / spread
    return (potential, scaled)


def solution(mesh):
    in_specs = (
        P(None, None, "lat", "lon"),
        P(),
        P("lat", "lon", None, None),
        P("lat", "lon", None),
        P("lat", "lon", None, None),
        P("lat", "lon", None, None, None, None),
    )
    out_specs = (P("lat", "lon"), P("lat", "lon"))
    return jax.shard_map(
        per_device, mesh=mesh, in_specs=in_specs, out_specs=out_specs, check_vma=False
    )
```

profile of v0, /device:TPU:0, one launch (start us, length us, event | category | flops | bytes accessed | tf_op | source)
XLA Modules:
  0.0 490.5 jit_solution(12209398333419576359)
XLA Ops:
  0.6 4.6 collective-permute-start
  13.6 5.1 %collective-permute-start.3 = (f32[1,514]{1,0:T(1,128)S(1)}, f32[1,514]{1,0:T(1,128)}, u32[]{:S(2)}, u32[]{:S(2)}) collective-permute-start(f32[1,514]{1,0:T(1,128)S(1)} %get-tuple-element.29), channel_id=1, source_target_pairs={{0,8},{8,16},{16,24},{1,9},{9,17},{17,25},{2,10},{10,18},{18,26},{... | collective-permute-start | bytes 6176 | tf_op jit(solution)/shard_map/ppermute | solution.py:20
  23.6 3.9 fusion.29
  32.7 4.3 all-to-all-start
  37.8 14.7 %all-to-all-done = bf16[8,8,32,128]{3,0,2,1:T(8,128)(2,1)} async-done(((bf16[8,8,32,128]{3,0,2,1:T(8,128)(2,1)}), bf16[8,8,32,128]{3,0,2,1:T(8,128)(2,1)}, u32[]{:S(2)}, u32[]{:S(2)}) %all-to-all-start) | async-done | bytes 524320 | tf_op jit(solution)/shard_map/all_to_all | solution.py:76
  52.4 6.9 %fusion.4 = f32[8,32,8,128]{3,2,1,0:T(8,128)} fusion(bf16[8,8,32,128]{3,0,2,1:T(8,128)(2,1)} %all-to-all-done, bf16[1,1,8,32,128,128]{5,4,3,2,1,0:T(8,128)(2,1)} %param.13), kind=kOutput, calls=%fused_computation.10 | convolution fusion | flops 67108864 | bytes 9961472 | tf_op jit(solution)/shard_map/fskp,skpq->skfq/dot_general | solution.py:77
  60.4 27.6 %scatter_fusion = f32[256,8,128]{2,1,0:T(8,128)} fusion(f32[256,8,128]{2,1,0:T(8,128)} %broadcast.62.clone, s32[256]{0:T(256)S(1)} %reshape.153, f32[256,8,128]{2,1,0:T(8,128)} %bitcast.46), kind=kCustom, calls=%fused_computation.3 | custom fusion | flops 262144 | bytes 3146752 | tf_op jit(solution)/shard_map/scatter-add | solution.py:79
  94.7 38.4 %psum.42 = f32[]{:T(128)} all-reduce(f32[]{:T(128)} %get-tuple-element.11), channel_id=1, replica_groups=mesh['lat'=4,'lon'=8] {'lat','lon'}, use_global_device_ids=true, to_apply=%region_3.5 | all-reduce | flops 1 | bytes 8 | tf_op jit(solution)/shard_map/psum | solution.py:88
  135.3 43.2 %psum.43 = f32[]{:T(128)} all-reduce(f32[]{:T(128)} %multiply_reduce_fusion.2), channel_id=1, replica_groups=mesh['lat'=4,'lon'=8] {'lat','lon'}, use_global_device_ids=true, to_apply=%region_5.7 | all-reduce | flops 1 | bytes 8 | tf_op jit(solution)/shard_map/psum | solution.py:90
  187.3 4.7 collective-permute-start.7
  197.1 3.9 fusion.26
  206.0 17.7 %all_to_all.15 = bf16[8,8,32,128]{3,0,2,1:T(8,128)(2,1)S(1)} all-to-all(bf16[8,8,32,128]{3,0,2,1:T(8,128)(2,1)S(1)} %broadcast_select_fusion.4), channel_id=1, replica_groups=mesh['lat'=4,'lon'=8] {'lon'}, dimensions={1} | all-to-all | bytes 1048576 | tf_op jit(solution)/shard_map/all_to_all | solution.py:76
  223.7 6.7 %fusion.2 = f32[8,32,8,128]{3,2,1,0:T(8,128)} fusion(bf16[8,8,32,128]{3,0,2,1:T(8,128)(2,1)S(1)} %all_to_all.15, bf16[1,1,8,32,128,128]{5,4,3,2,1,0:T(8,128)(2,1)} %param.13), kind=kOutput, calls=%fused_computation.8 | convolution fusion | flops 67108864 | bytes 9961472 | tf_op jit(solution)/shard_map/fskp,skpq->skfq/dot_general | solution.py:77
  231.5 27.6 %scatter_fusion.1 = f32[256,8,128]{2,1,0:T(8,128)} fusion(f32[256,8,128]{2,1,0:T(8,128)} %broadcast.62.clone.1, s32[256]{0:T(256)S(1)} %reshape.153, f32[256,8,128]{2,1,0:T(8,128)} %bitcast.47), kind=kCustom, calls=%fused_computation.4 | custom fusion | flops 262144 | bytes 3146752 | tf_op jit(solution)/shard_map/scatter-add | solution.py:79
  263.3 39.7 %psum.44 = f32[]{:T(128)} all-reduce(f32[]{:T(128)} %get-tuple-element.7), channel_id=1, replica_groups=mesh['lat'=4,'lon'=8] {'lat','lon'}, use_global_device_ids=true, to_apply=%region_9.11 | all-reduce | flops 1 | bytes 8 | tf_op jit(solution)/shard_map/psum | solution.py:88
  304.3 42.5 %psum.45 = f32[]{:T(128)} all-reduce(f32[]{:T(128)} %multiply_reduce_fusion.1), channel_id=1, replica_groups=mesh['lat'=4,'lon'=8] {'lat','lon'}, use_global_device_ids=true, to_apply=%region_11.13 | all-reduce | flops 1 | bytes 8 | tf_op jit(solution)/shard_map/psum | solution.py:90
  350.6 3.5 collective-permute-done.9
  355.4 4.5 collective-permute-start.11
  364.4 3.9 fusion.23
  371.6 17.7 %all_to_all.16 = bf16[8,8,32,128]{3,0,2,1:T(8,128)(2,1)S(1)} all-to-all(bf16[8,8,32,128]{3,0,2,1:T(8,128)(2,1)S(1)} %broadcast_select_fusion.3), channel_id=1, replica_groups=mesh['lat'=4,'lon'=8] {'lon'}, dimensions={1} | all-to-all | bytes 1048576 | tf_op jit(solution)/shard_map/all_to_all | solution.py:76
  389.4 4.7 fusion
  394.2 8.3 %scatter_fusion.2 = f32[256,8,128]{2,1,0:T(8,128)S(1)} fusion(f32[256,8,128]{2,1,0:T(8,128)S(1)} %broadcast.62, s32[256]{0:T(256)S(1)} %reshape.153, f32[256,8,128]{2,1,0:T(8,128)S(1)} %bitcast.45), kind=kCustom, calls=%fused_computation.5 | custom fusion | flops 262144 | bytes 3146752 | tf_op jit(solution)/shard_map/scatter-add | solution.py:79
  405.0 40.3 %psum.46 = f32[]{:T(128)} all-reduce(f32[]{:T(128)} %get-tuple-element.3), channel_id=1, replica_groups=mesh['lat'=4,'lon'=8] {'lat','lon'}, use_global_device_ids=true, to_apply=%region_15.17 | all-reduce | flops 1 | bytes 8 | tf_op jit(solution)/shard_map/psum | solution.py:88
  446.5 42.5 %psum.47 = f32[]{:T(128)} all-reduce(f32[]{:T(128)} %multiply_reduce_fusion), channel_id=1, replica_groups=mesh['lat'=4,'lon'=8] {'lat','lon'}, use_global_device_ids=true, to_apply=%region_17.19 | all-reduce | flops 1 | bytes 8 | tf_op jit(solution)/shard_map/psum | solution.py:90
  (107 shorter events, 68.5 us)
Async XLA Ops:
  0.6 10.9 %collective-permute-start = (f32[64,1]{1,0:T(8,128)S(1)}, f32[64,1]{1,0:T(8,128)S(1)}, u32[]{:S(2)}, u32[]{:S(2)}) collective-permute-start(f32[64,1]{1,0:T(8,128)S(1)} %broadcast.60), channel_id=1, source_target_pairs={{1,0},{2,1},{3,2},{4,3},{5,4},{6,5},{7,6},{0,7},{9,8},{10,9},{11,1... | collective-permute-start | bytes 776 | tf_op jit(solution)/shard_map/ppermute | solution.py:21
  5.2 6.3 %collective-permute-start.1 = (f32[64,1]{1,0:T(8,128)S(1)}, f32[64,1]{1,0:T(8,128)S(1)}, u32[]{:S(2)}, u32[]{:S(2)}) collective-permute-start(f32[64,1]{1,0:T(8,128)S(1)} %broadcast.60), channel_id=1, source_target_pairs={{0,1},{1,2},{2,3},{3,4},{4,5},{5,6},{6,7},{7,0},{8,9},{9,10},{10,1... | collective-permute-start | bytes 776 | tf_op jit(solution)/shard_map/ppermute | solution.py:20
  10.1 22.7 %copy-start.9 = (pred[8,32]{1,0:T(8,128)(4,1)}, pred[8,32]{1,0:T(8,128)(4,1)S(1)}, u32[]{:S(2)}) copy-start(pred[8,32]{1,0:T(8,128)(4,1)S(1)} %iota_compare_fusion) | copy-start | bytes 772
  11.5 7.9 %copy-start.8 = (f32[64,1]{1,0:T(8,128)}, f32[64,1]{1,0:T(8,128)S(1)}, u32[]{:S(2)}) copy-start(f32[64,1]{1,0:T(8,128)S(1)} %collective-permute-done.1) | copy-start | bytes 772
  12.3 7.2 %collective-permute-start.2 = (f32[1,514]{1,0:T(1,128)S(1)}, f32[1,514]{1,0:T(1,128)S(1)}, u32[]{:S(2)}, u32[]{:S(2)}) collective-permute-start(f32[1,514]{1,0:T(1,128)S(1)} %get-tuple-element.28), channel_id=1, source_target_pairs={{8,0},{16,8},{24,16},{9,1},{17,9},{25,17},{10,2},{18,10},{26,18},{... | collective-permute-start | bytes 6176 | tf_op jit(solution)/shard_map/ppermute | solution.py:21
  13.6 6.5 %collective-permute-start.3 = (f32[1,514]{1,0:T(1,128)S(1)}, f32[1,514]{1,0:T(1,128)}, u32[]{:S(2)}, u32[]{:S(2)}) collective-permute-start(f32[1,514]{1,0:T(1,128)S(1)} %get-tuple-element.29), channel_id=1, source_target_pairs={{0,8},{8,16},{16,24},{1,9},{9,17},{17,25},{2,10},{10,18},{18,26},{... | collective-permute-start | bytes 6176 | tf_op jit(solution)/shard_map/ppermute | solution.py:20
  32.7 19.7 %all-to-all-start = ((bf16[8,8,32,128]{3,0,2,1:T(8,128)(2,1)}), bf16[8,8,32,128]{3,0,2,1:T(8,128)(2,1)}, u32[]{:S(2)}, u32[]{:S(2)}) async-start(bf16[8,8,32,128]{3,0,2,1:T(8,128)(2,1)} %broadcast_select_fusion.5), calls=%async_computation | async-start | bytes 1048576 | tf_op jit(solution)/shard_map/all_to_all | solution.py:76
  180.3 2.1 collective-permute-start.4
  180.8 5.1 %collective-permute-start.5 = (f32[64,1]{1,0:T(8,128)S(1)}, f32[64,1]{1,0:T(8,128)S(1)}, u32[]{:S(2)}, u32[]{:S(2)}) collective-permute-start(f32[64,1]{1,0:T(8,128)S(1)} %get-tuple-element.34), channel_id=1, source_target_pairs={{0,1},{1,2},{2,3},{3,4},{4,5},{5,6},{6,7},{7,0},{8,9},{9,10},{10,1... | collective-permute-start | bytes 776 | tf_op jit(solution)/shard_map/ppermute | solution.py:20
  182.5 47.9 %copy-start.6 = (f32[64,1]{1,0:T(8,128)}, f32[64,1]{1,0:T(8,128)S(1)}, u32[]{:S(2)}) copy-start(f32[64,1]{1,0:T(8,128)S(1)} %collective-permute-done.4) | copy-start | bytes 772
  185.9 44.5 %copy-start.7 = (f32[64,1]{1,0:T(8,128)}, f32[64,1]{1,0:T(8,128)S(1)}, u32[]{:S(2)}) copy-start(f32[64,1]{1,0:T(8,128)S(1)} %collective-permute-done.5) | copy-start | bytes 772
  186.0 7.8 %collective-permute-start.6 = (f32[1,514]{1,0:T(1,128)S(1)}, f32[1,514]{1,0:T(1,128)S(1)}, u32[]{:S(2)}, u32[]{:S(2)}) collective-permute-start(f32[1,514]{1,0:T(1,128)S(1)} %get-tuple-element.24), channel_id=1, source_target_pairs={{8,0},{16,8},{24,16},{9,1},{17,9},{25,17},{10,2},{18,10},{26,18},{... | collective-permute-start | bytes 6176 | tf_op jit(solution)/shard_map/ppermute | solution.py:21
  187.3 6.5 %collective-permute-start.7 = (f32[1,514]{1,0:T(1,128)S(1)}, f32[1,514]{1,0:T(1,128)S(1)}, u32[]{:S(2)}, u32[]{:S(2)}) collective-permute-start(f32[1,514]{1,0:T(1,128)S(1)} %get-tuple-element.25), channel_id=1, source_target_pairs={{0,8},{8,16},{16,24},{1,9},{9,17},{17,25},{2,10},{10,18},{18,26},{... | collective-permute-start | bytes 6176 | tf_op jit(solution)/shard_map/ppermute | solution.py:20
  194.0 0.7 copy-start.2
  194.0 0.7 copy-start.3
  223.7 35.4 %copy-start.11 = (f32[8]{0:T(128)S(1)}, f32[8]{0:T(128)}, u32[]{:S(2)}) copy-start(f32[8]{0:T(128)} %param.9) | copy-start | bytes 100
  231.5 139.8 %copy-start.10 = (pred[8,32]{1,0:T(8,128)(4,1)S(1)}, pred[8,32]{1,0:T(8,128)(4,1)}, u32[]{:S(2)}) copy-start(pred[8,32]{1,0:T(8,128)(4,1)} %copy-done.9) | copy-start | bytes 772
  263.3 84.1 %copy-start.5 = (f32[64,512]{1,0:T(8,128)}, f32[64,512]{1,0:T(8,128)S(1)}, u32[]{:S(2)}) copy-start(f32[64,512]{1,0:T(8,128)S(1)} %get-tuple-element.8) | copy-start | bytes 393220
  348.5 2.1 collective-permute-start.8
  348.9 5.1 %collective-permute-start.9 = (f32[64,1]{1,0:T(8,128)S(1)}, f32[64,1]{1,0:T(8,128)S(1)}, u32[]{:S(2)}, u32[]{:S(2)}) collective-permute-start(f32[64,1]{1,0:T(8,128)S(1)} %get-tuple-element.32), channel_id=1, source_target_pairs={{0,1},{1,2},{2,3},{3,4},{4,5},{5,6},{6,7},{7,0},{8,9},{9,10},{10,1... | collective-permute-start | bytes 776 | tf_op jit(solution)/shard_map/ppermute | solution.py:20
  354.1 6.7 %collective-permute-start.10 = (f32[1,514]{1,0:T(1,128)S(1)}, f32[1,514]{1,0:T(1,128)S(1)}, u32[]{:S(2)}, u32[]{:S(2)}) collective-permute-start(f32[1,514]{1,0:T(1,128)S(1)} %get-tuple-element.20), channel_id=1, source_target_pairs={{8,0},{16,8},{24,16},{9,1},{17,9},{25,17},{10,2},{18,10},{26,18},{... | collective-permute-start | bytes 6176 | tf_op jit(solution)/shard_map/ppermute | solution.py:21
  355.4 5.8 %collective-permute-start.11 = (f32[1,514]{1,0:T(1,128)S(1)}, f32[1,514]{1,0:T(1,128)S(1)}, u32[]{:S(2)}, u32[]{:S(2)}) collective-permute-start(f32[1,514]{1,0:T(1,128)S(1)} %get-tuple-element.21), channel_id=1, source_target_pairs={{0,8},{8,16},{16,24},{1,9},{9,17},{17,25},{2,10},{10,18},{18,26},{... | collective-permute-start | bytes 6176 | tf_op jit(solution)/shard_map/ppermute | solution.py:20
  361.4 0.7 copy-start.1
  389.4 13.1 %copy-start = (f32[8,256,128]{2,0,1:T(8,128)S(1)}, f32[8,256,128]{2,0,1:T(8,128)}, u32[]{:S(2)}) copy-start(f32[8,256,128]{2,0,1:T(8,128)} %get-tuple-element.6) | copy-start | bytes 3145732
  (2 other events, 1.2 us)
where the time goes:
time: 494 us; the launch traced here: 490 us
  blocking collectives  282 us (57%)
  other arithmetic  108 us (22%)
  starting transfers between devices  28.1 us (6%)
  waiting for transfers between devices  25.2 us (5%)
  local copies, waits for them, and re-layouts  23.7 us (5%)
  matrix products  18.3 us (4%)
  between operations  4.99 us (1%)
    psum x3, blocking collectives, per_device(): lax.psum(jnp.sum(residual * residual), ('lat', 'lon')) / cell_total  128 us
    psum x3, blocking collectives, per_device(): target = lax.psum(jnp.sum(balance), ('lat', 'lon')) / cell_total  118 us
    scatter-add x3, other arithmetic, per_device(): summed = jax.ops.segment_sum(contrib, target_ids, num_segments=TILES)  63.5 us
    all_to_all x2, blocking collectives, per_device(): lax.all_to_all(picked, 'lon', split_axis=1, concat_axis=1, tiled=True)  35.5 us
    dot_general x3, matrix products, per_device(): jnp.einsum('fskp,skpq->skfq', picked, blocks, preferred_element_type=jnp....  18.3 us
    all_to_all x1, waiting for transfers between devices, per_device(): lax.all_to_all(picked, 'lon', split_axis=1, concat_axis=1, tiled=True)  14.7 us
    ppermute x6, starting transfers between devices, extended(): before = lax.ppermute(last, axis, up)  14.6 us
    convert_element_type x3, other arithmetic, per_device(): sent = displaced_nodes.astype(jnp.bfloat16)  11.8 us
  transfers between devices with their start and end apart: 13, of which 6 were waited for; matrix products, arithmetic and copies ran while one was open for 2% of the time, Pallas kernels for 0%

commit v1 on v0

v1 whole, which is shorter than its diff:
```python
import functools

import jax
import jax.numpy as jnp
from jax import lax
from jax.experimental import pallas as pl
from jax.experimental.pallas import tpu as pltpu
from jax.sharding import PartitionSpec as P

FIELDS = 8
TILE = 128
CAP = 32
SWEEPS = 3

VMEM = pltpu.MemorySpace.VMEM
SMEM = pltpu.MemorySpace.SMEM


def pack_tiles(ids_ref, occ_ref, moved_ref, send_ref, rows, blocks):
    def one_dest(d, carry):
        count = occ_ref[d]
        for k in range(CAP):
            tile = ids_ref[d, k]
            row = lax.div(tile, blocks)
            block = lax.rem(tile, blocks)
            values = moved_ref[block, pl.ds(row, FIELDS, stride=rows), :]
            values = jnp.where(k < count, values, jnp.zeros_like(values))
            send_ref[d, k] = values.astype(jnp.bfloat16)
        return carry

    lax.fori_loop(0, ids_ref.shape[0], one_dest, 0)


def first_kernel(ids_ref, occ_ref, pq_ref, moved_ref, send_ref):
    rows, cols = pq_ref.shape[1:]
    blocks = cols // TILE
    for c in range(blocks):
        for f in range(FIELDS):
            moved_ref[c, f * rows : (f + 1) * rows, :] = pq_ref[
                f, :, c * TILE : (c + 1) * TILE
            ].astype(jnp.float32)
    pack_tiles(ids_ref, occ_ref, moved_ref, send_ref, rows, blocks)


def column_to_lanes(column, offset):
    rows = column.shape[0]
    row_id = lax.broadcasted_iota(jnp.int32, (rows, TILE), 0)
    lane_id = lax.broadcasted_iota(jnp.int32, (rows, TILE), 1)
    wide = jnp.broadcast_to(column, (rows, TILE))
    return jnp.sum(jnp.where(lane_id == row_id + offset, wide, 0.0), axis=0, keepdims=True)


def lanes_to_column(lanes, rows, offset):
    row_id = lax.broadcasted_iota(jnp.int32, (rows, TILE), 0)
    lane_id = lax.broadcasted_iota(jnp.int32, (rows, TILE), 1)
    wide = jnp.broadcast_to(lanes, (rows, TILE))
    return jnp.sum(jnp.where(lane_id == row_id + offset, wide, 0.0), axis=1, keepdims=True)


def lane_value(lanes, index):
    lane_id = lax.broadcasted_iota(jnp.int32, lanes.shape, 1)
    return jnp.sum(jnp.where(lane_id == index, lanes, 0.0), axis=1, keepdims=True)


def mesh_place():
    lat, lon = lax.axis_index("lat"), lax.axis_index("lon")
    return lat, lon


def interp_kernel(n_lat, n_lon, has_det, *refs):
    targets_ref, coef_ref, x_ref, w_hbm, moved_ref = refs[:5]
    refs = refs[5:]
    det_ref = None
    if has_det:
        det_ref, refs = refs[0], refs[1:]
    monitor_ref, balance_ref, pay_ref, w_ref, acc_ref, sems = refs
    rows, cols = monitor_ref.shape
    blocks = cols // TILE

    def fetch(s):
        return pltpu.make_async_copy(w_hbm.at[s], w_ref.at[s], sems.at[s])

    for s in range(n_lon):
        fetch(s).start()
    acc_ref[...] = jnp.zeros_like(acc_ref)

    def one_source(s, carry):
        fetch(s).wait()
        for k in range(CAP):
            out = jnp.dot(x_ref[s, k], w_ref[s, k], preferred_element_type=jnp.float32)
            place = pl.ds(pl.multiple_of(targets_ref[s, k] * FIELDS, FIELDS), FIELDS)
            acc_ref[place, :] += out
        return carry

    lax.fori_loop(0, n_lon, one_source, 0)

    for c in range(blocks):
        for b in range(rows // 8):
            total = jnp.ones((8, TILE), jnp.float32)
            for f in range(FIELDS):
                start = (b * 8 * blocks + c) * FIELDS + f
                interp = acc_ref[pl.ds(start, 8, stride=blocks * FIELDS), :]
                blended = moved_ref[c, f * rows + b * 8 : f * rows + b * 8 + 8, :] + interp
                total = total + coef_ref[f] * (blended * blended)
            monitor_ref[b * 8 : b * 8 + 8, c * TILE : (c + 1) * TILE] = jnp.sqrt(total)

    monitor = monitor_ref[...]
    if has_det:
        det = det_ref[...]
        balance = monitor * det
    else:
        det = jnp.ones((rows, cols), jnp.float32)
        balance = monitor
    balance_ref[...] = balance
    inverse = 1.0 / monitor
    count = rows * cols
    mean = jnp.sum(jnp.sum(balance, axis=0, keepdims=True), axis=1, keepdims=True) / count
    away = balance - mean
    squares = jnp.sum(jnp.sum(away * away, axis=0, keepdims=True), axis=1, keepdims=True)
    lane_id = lax.broadcasted_iota(jnp.int32, (1, TILE), 1)
    stats = jnp.where(lane_id == 0, mean, jnp.where(lane_id == 1, squares, 0.0))
    for j in range(n_lat * n_lon):
        pay_ref[j, :, 2 * cols : 2 * cols + TILE] = stats

    lat, lon = mesh_place()
    left = lax.rem(lon + n_lon - 1, n_lon)
    right = lax.rem(lon + 1, n_lon)
    for side, col in ((left, 0), (right, cols - 1)):
        lanes = column_to_lanes(det[:, col : col + 1], 0)
        lanes = lanes + column_to_lanes(inverse[:, col : col + 1], rows)
        pay_ref[lat * n_lon + side, :, 0:TILE] = lanes

    def send_row(other, row):
        pay_ref[other * n_lon + lon, :, 0:cols] = det[row : row + 1, :]
        pay_ref[other * n_lon + lon, :, cols : 2 * cols] = inverse[row : row + 1, :]
        for side, col in ((left, 0), (right, cols - 1)):
            lanes = jnp.where(
                lane_id == 0,
                det[row : row + 1, col : col + 1],
                inverse[row : row + 1, col : col + 1],
            )
            pay_ref[other * n_lon + side, :, 0:TILE] = lanes

    @pl.when(lat > 0)
    def _():
        send_row(lat - 1, 0)

    @pl.when(lat < n_lat - 1)
    def _():
        send_row(lat + 1, rows - 1)


def whole_stats(got_ref, n_dev, count, stat_at):
    total = got_ref[0, :, stat_at : stat_at + TILE]
    for j in range(1, n_dev):
        total = total + got_ref[j, :, stat_at : stat_at + TILE]
    target = lane_value(total, 0) / n_dev
    apart = jnp.zeros((1, TILE), jnp.float32)
    for j in range(n_dev):
        away = got_ref[j, :, stat_at : stat_at + TILE] - target
        apart = apart + away * away
    variance = (lane_value(total, 1) / count + lane_value(apart, 0)) / n_dev
    return target, jnp.sqrt(variance + 1e-06)


def update_kernel(n_lat, n_lon, n_got, *refs):
    ids_ref, occ_ref = refs[:2]
    got_refs = refs[2 : 2 + n_got]
    refs = refs[2 + n_got :]
    if n_got > 1:
        old_ref, refs = refs[0], refs[1:]
    monitor_ref, balance_ref, pq_ref, pot_ref, det_ref, moved_ref, send_ref = refs
    rows, cols = monitor_ref.shape
    blocks = cols // TILE
    n_dev = n_lat * n_lon
    lat, lon = mesh_place()
    left = lax.rem(lon + n_lon - 1, n_lon)
    right = lax.rem(lon + 1, n_lon)
    below = jnp.maximum(lat - 1, 0)
    above = jnp.minimum(lat + 1, n_lat - 1)

    south_row = jnp.zeros((1, cols), jnp.float32)
    north_row = jnp.zeros((1, cols), jnp.float32)
    sides = [jnp.zeros((rows, 1), jnp.float32)] * 2
    corners = [jnp.zeros((1, 1), jnp.float32)] * 4
    for got_ref in got_refs:
        target, spread = whole_stats(got_ref, n_dev, rows * cols, 2 * cols)

        def gain(det, inverse):
            return 0.5 * (det - target * inverse) / spread

        def row_from(j):
            return gain(got_ref[j, :, 0:cols], got_ref[j, :, cols : 2 * cols])

        south_row = south_row + row_from(below * n_lon + lon)
        north_row = north_row + row_from(above * n_lon + lon)
        for i, side in enumerate((left, right)):
            lanes = got_ref[lat * n_lon + side, :, 0:TILE]
            sides[i] = sides[i] + gain(
                lanes_to_column(lanes, rows, 0), lanes_to_column(lanes, rows, rows)
            )
        for i, (other, side) in enumerate(
            ((below, left), (below, right), (above, left), (above, right))
        ):
            lanes = got_ref[other * n_lon + side, :, 0:TILE]
            corners[i] = corners[i] + gain(lane_value(lanes, 0), lane_value(lanes, 1))

    has_south, has_north = lat > 0, lat < n_lat - 1
    south_row = jnp.where(has_south, south_row, 0.0)
    north_row = jnp.where(has_north, north_row, 0.0)
    corners = [
        jnp.where(has, corner, 0.0)
        for has, corner in zip((has_south, has_south, has_north, has_north), corners)
    ]

    potential = 0.5 * (balance_ref[...] - target) / (monitor_ref[...] * spread)
    if n_got > 1:
        potential = old_ref[...] + potential
    pot_ref[...] = potential

    row_id = lax.broadcasted_iota(jnp.int32, (rows, cols), 0)
    lane_id = lax.broadcasted_iota(jnp.int32, (rows, cols), 1)
    first, last = row_id == 0, row_id == rows - 1
    west_edge, east_edge = lane_id == 0, lane_id == cols - 1
    north = jnp.where(last, north_row, pltpu.roll(potential, rows - 1, 0))
    south = jnp.where(first, south_row, pltpu.roll(potential, 1, 0))
    east = jnp.where(east_edge, sides[1], pltpu.roll(potential, cols - 1, 1))
    west = jnp.where(west_edge, sides[0], pltpu.roll(potential, 1, 1))
    zonal = (east - west) * 0.5
    tall = north - south
    meridional = tall * 0.5

    for c in range(blocks):
        lanes = slice(c * TILE, (c + 1) * TILE)
        for f in range(FIELDS):
            value = (
                pq_ref[0, f, :, lanes].astype(jnp.float32)
                + zonal[:, lanes] * pq_ref[1, f, :, lanes].astype(jnp.float32)
                + meridional[:, lanes] * pq_ref[2, f, :, lanes].astype(jnp.float32)
            )
            moved_ref[c, f * rows : (f + 1) * rows, :] = value
    pack_tiles(ids_ref, occ_ref, moved_ref, send_ref, rows, blocks)

    small_row = lax.broadcasted_iota(jnp.int32, (rows, TILE), 0)

    def side_tall(column, low, high):
        wide = jnp.broadcast_to(column, (rows, TILE))
        up = jnp.where(small_row == rows - 1, high, pltpu.roll(wide, rows - 1, 0))
        down = jnp.where(small_row == 0, low, pltpu.roll(wide, 1, 0))
        return (up - down)[:, 0:1]

    west_tall = side_tall(sides[0], corners[0], corners[2])
    east_tall = side_tall(sides[1], corners[1], corners[3])
    tall_east = jnp.where(east_edge, east_tall, pltpu.roll(tall, cols - 1, 1))
    tall_west = jnp.where(west_edge, west_tall, pltpu.roll(tall, 1, 1))
    mixed = (tall_east - tall_west) * 0.25
    second_lon = east - 2.0 * potential + west
    second_lat = north - 2.0 * potential + south
    det_ref[...] = (1.0 + second_lon) * (1.0 + second_lat) - mixed * mixed


def last_kernel(n_dev, got_ref, old_ref, monitor_ref, balance_ref, pot_ref, scaled_ref):
    rows, cols = monitor_ref.shape
    target, spread = whole_stats(got_ref, n_dev, rows * cols, 0)
    residual = balance_ref[...] - target
    scaled_ref[...] = residual / spread
    pot_ref[...] = old_ref[...] + 0.5 * residual / (monitor_ref[...] * spread)


def per_device(pq, coef, departing, occupancy, arriving, blocks_w):
    n_lat, n_lon = lax.axis_size("lat"), lax.axis_size("lon")
    n_dev = n_lat * n_lon
    rows, cols = pq.shape[2:]
    ids = departing[0, 0]
    occ = occupancy[0, 0]
    targets = arriving[0, 0]
    weights = blocks_w[0, 0]
    smem = pl.BlockSpec(memory_space=SMEM)
    vmem = pl.BlockSpec(memory_space=VMEM)
    hbm = pl.BlockSpec(memory_space=pl.ANY)
    f32 = jnp.float32
    grid = jax.ShapeDtypeStruct((rows, cols), f32)
    moved_shape = jax.ShapeDtypeStruct((cols // TILE, FIELDS * rows, TILE), f32)
    send_shape = jax.ShapeDtypeStruct((n_lon, CAP, FIELDS, TILE), jnp.bfloat16)
    pay_shape = jax.ShapeDtypeStruct((n_dev, 1, 2 * cols + TILE), f32)
    params = pltpu.CompilerParams(vmem_limit_bytes=48 << 20)

    moved, send = pl.pallas_call(
        first_kernel,
        out_shape=(moved_shape, send_shape),
        grid=(1,),
        in_specs=[
            smem,
            smem,
            pl.BlockSpec((pl.Squeezed(), FIELDS, rows, cols), lambda i: (0, 0, 0, 0)),
        ],
        out_specs=(
            pl.BlockSpec(moved_shape.shape, lambda i: (0, 0, 0)),
            pl.BlockSpec(send_shape.shape, lambda i: (0, 0, 0, 0)),
        ),
        compiler_params=params,
        name="first",
    )(ids, occ, pq)

    def interp(send, moved, det):
        got = lax.all_to_all(send, "lon", 0, 0, tiled=True)
        args = [targets, coef, got, weights, moved]
        specs = [smem, smem, vmem, hbm, vmem]
        if det is not None:
            args.append(det)
            specs.append(vmem)
        return pl.pallas_call(
            functools.partial(interp_kernel, n_lat, n_lon, det is not None),
            out_shape=(grid, grid, pay_shape),
            in_specs=specs,
            out_specs=(vmem, vmem, vmem),
            scratch_shapes=[
                pltpu.VMEM((n_lon, CAP, TILE, TILE), jnp.bfloat16),
                pltpu.VMEM((FIELDS * rows * cols // TILE, TILE), f32),
                pltpu.SemaphoreType.DMA((n_lon,)),
            ],
            compiler_params=params,
            name="interp",
        )(*args)

    def share(pay):
        return lax.all_to_all(pay, ("lat", "lon"), 0, 0, tiled=True)

    gots = []
    potential = det = None
    for sweep in range(SWEEPS):
        monitor, balance, pay = interp(send, moved, det)
        if sweep == SWEEPS - 1:
            break
        gots.append(share(pay))
        olds = [] if potential is None else [potential]
        potential, det, moved, send = pl.pallas_call(
            functools.partial(update_kernel, n_lat, n_lon, len(gots)),
            out_shape=(grid, grid, moved_shape, send_shape),
            in_specs=[smem, smem] + [vmem] * (len(gots) + len(olds) + 3),
            out_specs=(vmem,) * 4,
            compiler_params=params,
            name="update",
        )(ids, occ, *gots, *olds, monitor, balance, pq)

    got = share(pay[:, :, 2 * cols :])
    return pl.pallas_call(
        functools.partial(last_kernel, n_dev),
        out_shape=(grid, grid),
        in_specs=[vmem] * 4,
        out_specs=(vmem, vmem),
        compiler_params=params,
        name="last",
    )(got, potential, monitor, balance)


def solution(mesh):
    in_specs = (
        P(None, None, "lat", "lon"),
        P(),
        P("lat", "lon", None, None),
        P("lat", "lon", None),
        P("lat", "lon", None, None),
        P("lat", "lon", None, None, None, None),
    )
    out_specs = (P("lat", "lon"), P("lat", "lon"))
    return jax.shard_map(
        per_device, mesh=mesh, in_specs=in_specs, out_specs=out_specs, check_vma=False
    )
```

time: 494 us -> 119 us (0.24)
  blocking collectives: 282 us -> 88 us
  other arithmetic: 108 us -> 0 us
  starting transfers between devices: 28.1 us -> 0 us
  Pallas kernels: 0 us -> 26.2 us
  waiting for transfers between devices: 25.2 us -> 0 us
  local copies, waits for them, and re-layouts: 23.7 us -> 4.12 us
  matrix products: 18.3 us -> 0 us
    psum x6 -> x0, blocking collectives: 247 us -> none  [the longest x3 128 us: per_device(): lax.psum(jnp.sum(residual * residual), ('lat', 'lon')) / cell_total]
    scatter-add x3 -> x0, other arithmetic: 63.5 us -> none  [per_device(): summed = jax.ops.segment_sum(contrib, target_ids, num_segments=TILES)]
    all_to_all x2 -> x6, blocking collectives: 35.5 us -> 88 us  [the longest x3 57 us: interp(): got = lax.all_to_all(send, 'lon', 0, 0, tiled=True)]
    pallas_call x0 -> x7, Pallas kernels: none -> 26.2 us  [the longest x3 17.8 us: interp(): pl.pallas_call(functools.partial(interp_kernel, n_lat, n_lon, det is not...]
    ppermute x12 -> x0, starting transfers between devices: 23.9 us -> none  [the longest x6 14.6 us: extended(): before = lax.ppermute(last, axis, up)]
    dot_general x3 -> x0, matrix products: 18.3 us -> none  [per_device(): jnp.einsum('fskp,skpq->skfq', picked, blocks, preferred_element_type=jnp....]
    all_to_all x1 -> x0, waiting for transfers between devices: 14.7 us -> none  [per_device(): lax.all_to_all(picked, 'lon', split_axis=1, concat_axis=1, tiled=True)]
    convert_element_type x4 -> x0, other arithmetic: 14.5 us -> none  [the longest x3 11.8 us: per_device(): sent = displaced_nodes.astype(jnp.bfloat16)]
  transfers between devices with their start and end apart: 13 -> 0, of which waited for: 6 -> 0; matrix products, arithmetic and copies ran while one was open for 2% -> 0% of each run, Pallas kernels for 0% -> 0%
where the time goes in v1:
time: 119 us
  blocking collectives  88 us (74%)
  Pallas kernels  26.2 us (22%)
  local copies, waits for them, and re-layouts  4.12 us (3%)
    all_to_all x3, blocking collectives, interp(): got = lax.all_to_all(send, 'lon', 0, 0, tiled=True)  57 us
    all_to_all x3, blocking collectives, share(): return lax.all_to_all(pay, ('lat', 'lon'), 0, 0, tiled=True)  31 us
    pallas_call x3, Pallas kernels, interp(): pl.pallas_call(functools.partial(interp_kernel, n_lat, n_lon, det is not...  17.8 us
    pallas_call x2, Pallas kernels, per_device(): pl.pallas_call(functools.partial(update_kernel, n_lat, n_lon, len(gots)),...  5.47 us
    unnamed x20, local copies, waits for them, and re-layouts  4.11 us

profile of v1, /device:TPU:0, one launch (start us, length us, event | category | flops | bytes accessed | tf_op | source)
XLA Modules:
  0.0 119.0 jit_solution(3361425875419794087)
XLA Ops:
  0.6 0.0 copy-start.7
  0.6 0.0 copy-start
  0.6 1.4 %copy-done = bf16[3,8,64,512]{3,2,1,0:T(8,128)(2,1)S(1)} copy-done((bf16[3,8,64,512]{3,2,1,0:T(8,128)(2,1)S(1)}, bf16[3,8,64,512]{3,2,1,0:T(8,128)(2,1)}, u32[]{:S(2)}) %copy-start) | copy-done | bytes 1572888
  2.1 0.7 copy-done.2
  2.7 0.7 copy-done.6
  3.4 2.0 %first.1 = (f32[4,512,128]{2,1,0:T(8,128)S(1)}, bf16[8,32,8,128]{3,2,1,0:T(8,128)(2,1)S(1)}) custom-call(s32[8,32]{1,0:T(8,128)S(1)} %bitcast.4, s32[8]{0:T(128)S(1)} %bitcast.10, bf16[3,8,64,512]{3,2,1,0:T(8,128)(2,1)S(1)} %copy-done), custom_call_target="tpu_custom_call" | custom-call | tf_op jit(solution)/shard_map/first/pallas_call | solution.py:288
  5.4 21.5 %all_to_all.30.refs_2_ = bf16[8,32,8,128]{3,2,1,0:T(8,128)(2,1)S(1)} all-to-all(bf16[8,32,8,128]{3,2,1,0:T(8,128)(2,1)S(1)} %get-tuple-element.21), channel_id=1, replica_groups=mesh['lat'=4,'lon'=8] {'lon'}, dimensions={0} | all-to-all | bytes 1048576 | tf_op jit(solution)/shard_map/all_to_all | solution.py:306
  26.8 0.7 copy-done.4
  27.5 0.7 copy-done.8
  28.2 5.9 %interp.3 = (f32[64,512]{1,0:T(8,128)S(1)}, f32[64,512]{1,0:T(8,128)S(1)}, f32[32,1,1152]{2,1,0:T(1,128)S(1)}) custom-call(s32[8,32]{1,0:T(8,128)S(1)} %bitcast.7, f32[8]{0:T(128)S(1)} %copy-done.8, bf16[8,32,8,128]{3,2,1,0:T(8,128)(2,1)S(1)} %all_to_all.30.refs_2_, bf16[8,32,128,128]{3,2,1,0:T(8,128)(2,1)} %bitcast.13, ...), custom_call_target="tpu_custom_call" | custom-call | tf_op jit(solution)/shard_map/interp/pallas_call | solution.py:312
  34.1 11.7 %all_to_all.31.refs_2_ = f32[32,1,1152]{2,1,0:T(1,128)S(1)} all-to-all(f32[32,1,1152]{2,1,0:T(1,128)S(1)} %get-tuple-element.23), channel_id=1, replica_groups=mesh['lat'=4,'lon'=8] {'lat','lon'}, dimensions={0} | all-to-all | bytes 294912 | tf_op jit(solution)/shard_map/all_to_all | solution.py:327
  45.8 0.0 copy-done.7
  45.8 0.0 copy-done.1
  45.8 0.0 copy-done.3
  45.9 2.7 %update.2 = (f32[64,512]{1,0:T(8,128)S(1)}, f32[64,512]{1,0:T(8,128)S(1)}, f32[4,512,128]{2,1,0:T(8,128)S(1)}, bf16[8,32,8,128]{3,2,1,0:T(8,128)(2,1)S(1)}) custom-call(s32[8,32]{1,0:T(8,128)S(1)} %bitcast.5, s32[8]{0:T(128)S(1)} %bitcast.11, f32[32,1,1152]{2,1,0:T(1,128)S(1)} %all_to_all.31.refs_2_, f32[64,512]{1,0:T(8,128)S(1)} %get-tuple-element.24.refs_3_, ...), custom_call_target="tpu_custom_call" | custom-call | tf_op jit(solution)/shard_map/update/pallas_call | solution.py:337
  48.6 17.7 %all_to_all.32.refs_2_ = bf16[8,32,8,128]{3,2,1,0:T(8,128)(2,1)S(1)} all-to-all(bf16[8,32,8,128]{3,2,1,0:T(8,128)(2,1)S(1)} %get-tuple-element.26), channel_id=1, replica_groups=mesh['lat'=4,'lon'=8] {'lon'}, dimensions={0} | all-to-all | bytes 1048576 | tf_op jit(solution)/shard_map/all_to_all | solution.py:306
  66.3 5.9 %interp.4 = (f32[64,512]{1,0:T(8,128)S(1)}, f32[64,512]{1,0:T(8,128)S(1)}, f32[32,1,1152]{2,1,0:T(1,128)S(1)}) custom-call(s32[8,32]{1,0:T(8,128)S(1)} %bitcast.8, f32[8]{0:T(128)S(1)} %copy-done.8, bf16[8,32,8,128]{3,2,1,0:T(8,128)(2,1)S(1)} %all_to_all.32.refs_2_, bf16[8,32,128,128]{3,2,1,0:T(8,128)(2,1)} %bitcast.14, ...), custom_call_target="tpu_custom_call" | custom-call | tf_op jit(solution)/shard_map/interp/pallas_call | solution.py:312
  72.3 10.3 %all_to_all.33.refs_3_ = f32[32,1,1152]{2,1,0:T(1,128)S(1)} all-to-all(f32[32,1,1152]{2,1,0:T(1,128)S(1)} %get-tuple-element.29), channel_id=1, replica_groups=mesh['lat'=4,'lon'=8] {'lat','lon'}, dimensions={0} | all-to-all | bytes 294912 | tf_op jit(solution)/shard_map/all_to_all | solution.py:327
  82.5 2.7 %update.3 = (f32[64,512]{1,0:T(8,128)S(1)}, f32[64,512]{1,0:T(8,128)S(1)}, f32[4,512,128]{2,1,0:T(8,128)S(1)}, bf16[8,32,8,128]{3,2,1,0:T(8,128)(2,1)S(1)}) custom-call(s32[8,32]{1,0:T(8,128)S(1)} %bitcast.6, s32[8]{0:T(128)S(1)} %bitcast.12, f32[32,1,1152]{2,1,0:T(1,128)S(1)} %all_to_all.31.refs_2_, f32[32,1,1152]{2,1,0:T(1,128)S(1)} %all_to_all.33.refs_3_, ...), custom_call_target="tpu_custom_call" | custom-call | tf_op jit(solution)/shard_map/update/pallas_call | solution.py:337
  85.3 17.7 %all_to_all.34.refs_2_ = bf16[8,32,8,128]{3,2,1,0:T(8,128)(2,1)S(1)} all-to-all(bf16[8,32,8,128]{3,2,1,0:T(8,128)(2,1)S(1)} %get-tuple-element.33), channel_id=1, replica_groups=mesh['lat'=4,'lon'=8] {'lon'}, dimensions={0} | all-to-all | bytes 1048576 | tf_op jit(solution)/shard_map/all_to_all | solution.py:306
  103.0 0.0 copy-done.9
  103.0 5.9 %interp.5 = (f32[64,512]{1,0:T(8,128)S(1)}, f32[64,512]{1,0:T(8,128)S(1)}, f32[32,1,1152]{2,1,0:T(1,128)S(1)}) custom-call(s32[8,32]{1,0:T(8,128)S(1)} %bitcast.9, f32[8]{0:T(128)S(1)} %copy-done.9, bf16[8,32,8,128]{3,2,1,0:T(8,128)(2,1)S(1)} %all_to_all.34.refs_2_, bf16[8,32,128,128]{3,2,1,0:T(8,128)(2,1)} %bitcast.15, ...), custom_call_target="tpu_custom_call" | custom-call | tf_op jit(solution)/shard_map/interp/pallas_call | solution.py:312
  109.0 9.1 %all_to_all.35.got_ref = f32[32,1,128]{2,1,0:T(1,128)S(1)} all-to-all(f32[32,1,128]{2,1,0:T(1,128)S(1)} %slice.3), channel_id=1, replica_groups=mesh['lat'=4,'lon'=8] {'lat','lon'}, dimensions={0} | all-to-all | bytes 32768 | tf_op jit(solution)/shard_map/all_to_all | solution.py:327
  118.1 0.9 last.1
  (10 shorter events, 0.0 us)
Async XLA Ops:
  0.6 45.2 %copy-start.7 = (s32[1,1,8]{2,1,0:T(1,128)S(1)}, s32[1,1,8]{2,1,0:T(1,128)}, u32[]{:S(2)}) copy-start(s32[1,1,8]{2,1,0:T(1,128)} %param.9) | copy-start | bytes 100
  0.6 1.4 %copy-start = (bf16[3,8,64,512]{3,2,1,0:T(8,128)(2,1)S(1)}, bf16[3,8,64,512]{3,2,1,0:T(8,128)(2,1)}, u32[]{:S(2)}) copy-start(bf16[3,8,64,512]{3,2,1,0:T(8,128)(2,1)} %refs_7_.1) | copy-start | bytes 4718596
  2.1 0.7 copy-start.2
  2.7 0.7 copy-start.6
  3.4 42.4 %copy-start.1 = (bf16[3,8,64,512]{3,2,1,0:T(8,128)(2,1)S(1)}, bf16[3,8,64,512]{3,2,1,0:T(8,128)(2,1)}, u32[]{:S(2)}) copy-start(bf16[3,8,64,512]{3,2,1,0:T(8,128)(2,1)} %refs_7_.1) | copy-start | bytes 4718596
  3.4 42.4 %copy-start.3 = (s32[1,1,8,32]{3,2,1,0:T(8,128)S(1)}, s32[1,1,8,32]{3,2,1,0:T(8,128)}, u32[]{:S(2)}) copy-start(s32[1,1,8,32]{3,2,1,0:T(8,128)} %param.8) | copy-start | bytes 3076
  26.8 0.7 copy-start.4
  27.5 0.7 copy-start.8
  45.8 57.2 %copy-start.5 = (s32[1,1,8,32]{3,2,1,0:T(8,128)S(1)}, s32[1,1,8,32]{3,2,1,0:T(8,128)}, u32[]{:S(2)}) copy-start(s32[1,1,8,32]{3,2,1,0:T(8,128)} %param.10) | copy-start | bytes 3076
  45.8 57.2 %copy-start.9 = (f32[8]{0:T(128)S(1)}, f32[8]{0:T(128)}, u32[]{:S(2)}) copy-start(f32[8]{0:T(128)} %refs_1_.5) | copy-start | bytes 100

commit v2 on v1

--- a/solution.py
+++ b/solution.py
@@ -16,30 +16,85 @@
 SMEM = pltpu.MemorySpace.SMEM
 
 
-def pack_tiles(ids_ref, occ_ref, moved_ref, send_ref, rows, blocks):
+def to_tiles(pq_ref, out_ref):
+    fields, rows, cols = pq_ref.shape
+    blocks = cols // TILE
+    for b in range(rows // 16):
+        for c in range(blocks):
+            part = pq_ref[:, b * 16 : b * 16 + 16, c * TILE : (c + 1) * TILE]
+            part = jnp.transpose(part.astype(jnp.float32), (1, 0, 2))
+            for i in range(16):
+                start = ((b * 16 + i) * blocks + c) * fields
+                out_ref[start : start + fields, :] = part[i]
+
+
+def pack_tiles(ids_ref, occ_ref, moved_ref, send_ref):
     def one_dest(d, carry):
         count = occ_ref[d]
-        for k in range(CAP):
-            tile = ids_ref[d, k]
-            row = lax.div(tile, blocks)
-            block = lax.rem(tile, blocks)
-            values = moved_ref[block, pl.ds(row, FIELDS, stride=rows), :]
-            values = jnp.where(k < count, values, jnp.zeros_like(values))
-            send_ref[d, k] = values.astype(jnp.bfloat16)
+        for k in range(0, CAP, 2):
+            pair = []
+            for i in (k, k + 1):
+                start = pl.multiple_of(ids_ref[d, i] * FIELDS, FIELDS)
+                values = moved_ref[pl.ds(start, FIELDS), :]
+                pair.append(jnp.where(i < count, values, jnp.zeros_like(values)))
+            place = pl.multiple_of((d * CAP + k) * FIELDS, 2 * FIELDS)
+            send_ref[pl.ds(place, 2 * FIELDS), :] = jnp.concatenate(pair, axis=0).astype(
+                jnp.bfloat16
+            )
         return carry
 
     lax.fori_loop(0, ids_ref.shape[0], one_dest, 0)
 
 
-def first_kernel(ids_ref, occ_ref, pq_ref, moved_ref, send_ref):
-    rows, cols = pq_ref.shape[1:]
-    blocks = cols // TILE
-    for c in range(blocks):
-        for f in range(FIELDS):
-            moved_ref[c, f * rows : (f + 1) * rows, :] = pq_ref[
-                f, :, c * TILE : (c + 1) * TILE
-            ].astype(jnp.float32)
-    pack_tiles(ids_ref, occ_ref, moved_ref, send_ref, rows, blocks)
+def first_kernel(early, *refs):
+    ids_hbm, occ_hbm, targets_hbm, coef_hbm, pq_hbm, w_hbm = refs[:6]
+    send_ref, still_ref, lon_ref, lat_ref, targets_ref, coef_ref, w_ref = refs[6:13]
+    ids_ref, occ_ref, pq_ref, sems = refs[13:]
+    fields = [
+        pltpu.make_async_copy(pq_hbm.at[i], pq_ref.at[i], sems.at[i]) for i in range(3)
+    ]
+    lists = [
+        pltpu.make_async_copy(ids_hbm, ids_ref, sems.at[3]),
+        pltpu.make_async_copy(occ_hbm, occ_ref, sems.at[4]),
+    ]
+    later = [
+        pltpu.make_async_copy(targets_hbm, targets_ref, sems.at[5]),
+        pltpu.make_async_copy(coef_hbm, coef_ref, sems.at[6]),
+        pltpu.make_async_copy(w_hbm.at[pl.ds(0, early)], w_ref, sems.at[7]),
+    ]
+    for copy in (fields[0], *lists, *fields[1:], *later):
+        copy.start()
+    fields[0].wait()
+    to_tiles(pq_ref.at[0], still_ref)
+    for copy in lists:
+        copy.wait()
+    pack_tiles(ids_ref, occ_ref, still_ref, send_ref)
+    for i, out_ref in ((1, lon_ref), (2, lat_ref)):
+        fields[i].wait()
+        to_tiles(pq_ref.at[i], out_ref)
+    for copy in later:
+        copy.wait()
+
+
+def sum_fields(tiles):
+    sub = lax.broadcasted_iota(jnp.int32, (8, TILE), 0)
+    high = (sub & 4) == 0
+    pairs = []
+    for i in range(4):
+        one, two = tiles[i], tiles[i + 4]
+        kept, moving = jnp.where(high, one, two), jnp.where(high, two, one)
+        pairs.append(kept + pltpu.roll(moving, 4, 0))
+    for step in (2, 1):
+        near = (sub & step) == 0
+        pairs = [
+            jnp.where(
+                near,
+                pairs[i] + pltpu.roll(pairs[i], 8 - step, 0),
+                pairs[i + step] + pltpu.roll(pairs[i + step], step, 0),
+            )
+            for i in range(step)
+        ]
+    return pairs[0]
 
 
 def column_to_lanes(column, offset):
@@ -67,50 +122,74 @@
     return lat, lon
 
 
-def interp_kernel(n_lat, n_lon, has_det, *refs):
-    targets_ref, coef_ref, x_ref, w_hbm, moved_ref = refs[:5]
-    refs = refs[5:]
-    det_ref = None
-    if has_det:
-        det_ref, refs = refs[0], refs[1:]
-    monitor_ref, balance_ref, pay_ref, w_ref, acc_ref, sems = refs
+def interp_kernel(n_lat, n_lon, early, start_sweep, *refs):
+    targets_ref, coef_ref, x_ref, early_ref, late_hbm, moved_ref = refs[:6]
+    if start_sweep:
+        monitor_ref, balance_ref, pay_ref, late_ref, acc_ref, sems = refs[6:]
+    else:
+        late_ref = late_hbm
+        det_ref, monitor_ref, balance_ref, pay_ref, acc_ref = refs[6:]
     rows, cols = monitor_ref.shape
     blocks = cols // TILE
 
     def fetch(s):
-        return pltpu.make_async_copy(w_hbm.at[s], w_ref.at[s], sems.at[s])
-
-    for s in range(n_lon):
-        fetch(s).start()
+        return pltpu.make_async_copy(late_hbm.at[early + s], late_ref.at[s], sems.at[s])
+
+    if start_sweep:
+        for s in range(n_lon - early):
+            fetch(s).start()
     acc_ref[...] = jnp.zeros_like(acc_ref)
 
-    def one_source(s, carry):
-        fetch(s).wait()
-        for k in range(CAP):
-            out = jnp.dot(x_ref[s, k], w_ref[s, k], preferred_element_type=jnp.float32)
-            place = pl.ds(pl.multiple_of(targets_ref[s, k] * FIELDS, FIELDS), FIELDS)
-            acc_ref[place, :] += out
+    def add_source(s, w_ref, first_source):
+        for k in range(0, CAP, 2):
+            slot = pl.multiple_of(((s + first_source) * CAP + k) * FIELDS, 2 * FIELDS)
+            pair = jnp.concatenate([w_ref[s, k], w_ref[s, k + 1]], axis=1)
+            out = jnp.dot(
+                x_ref[pl.ds(slot, 2 * FIELDS), :], pair, preferred_element_type=jnp.float32
+            )
+            for i in (0, 1):
+                target = targets_ref[s + first_source, k + i]
+                place = pl.ds(pl.multiple_of(target * FIELDS, FIELDS), FIELDS)
+                acc_ref[place, :] += out[
+                    i * FIELDS : (i + 1) * FIELDS, i * TILE : (i + 1) * TILE
+                ]
+
+    def one_early(s, carry):
+        add_source(s, early_ref, 0)
         return carry
 
-    lax.fori_loop(0, n_lon, one_source, 0)
-
-    for c in range(blocks):
-        for b in range(rows // 8):
-            total = jnp.ones((8, TILE), jnp.float32)
-            for f in range(FIELDS):
-                start = (b * 8 * blocks + c) * FIELDS + f
-                interp = acc_ref[pl.ds(start, 8, stride=blocks * FIELDS), :]
-                blended = moved_ref[c, f * rows + b * 8 : f * rows + b * 8 + 8, :] + interp
-                total = total + coef_ref[f] * (blended * blended)
-            monitor_ref[b * 8 : b * 8 + 8, c * TILE : (c + 1) * TILE] = jnp.sqrt(total)
+    def one_late(s, carry):
+        if start_sweep:
+            fetch(s).wait()
+        add_source(s, late_ref, early)
+        return carry
+
+    lax.fori_loop(0, early, one_early, 0)
+    lax.fori_loop(0, n_lon - early, one_late, 0)
+
+    field_id = lax.broadcasted_iota(jnp.int32, (FIELDS, TILE), 0)
+    coef = jnp.zeros((FIELDS, TILE), jnp.float32)
+    for f in range(FIELDS):
+        coef = jnp.where(field_id == f, coef_ref[f], coef)
+    for b in range(rows // 8):
+        for c in range(blocks):
+            parts = []
+            for i in range(8):
+                start = ((b * 8 + i) * blocks + c) * FIELDS
+                place = slice(start, start + FIELDS)
+                blended = moved_ref[place, :] + acc_ref[place, :]
+                parts.append(coef * (blended * blended))
+            monitor_ref[b * 8 : b * 8 + 8, c * TILE : (c + 1) * TILE] = jnp.sqrt(
+                1.0 + sum_fields(parts)
+            )
 
     monitor = monitor_ref[...]
-    if has_det:
+    if start_sweep:
+        det = jnp.ones((rows, cols), jnp.float32)
+        balance = monitor
+    else:
         det = det_ref[...]
         balance = monitor * det
-    else:
-        det = jnp.ones((rows, cols), jnp.float32)
-        balance = monitor
     balance_ref[...] = balance
     inverse = 1.0 / monitor
     count = rows * cols
@@ -169,7 +248,19 @@
     refs = refs[2 + n_got :]
     if n_got > 1:
         old_ref, refs = refs[0], refs[1:]
-    monitor_ref, balance_ref, pq_ref, pot_ref, det_ref, moved_ref, send_ref = refs
+    (
+        monitor_ref,
+        balance_ref,
+        still_ref,
+        lon_ref,
+        lat_ref,
+        pot_ref,
+        det_ref,
+        moved_ref,
+        send_ref,
+        zonal_ref,
+        meridional_ref,
+    ) = refs
     rows, cols = monitor_ref.shape
     blocks = cols // TILE
     n_dev = n_lat * n_lon
@@ -226,20 +317,23 @@
     south = jnp.where(first, south_row, pltpu.roll(potential, 1, 0))
     east = jnp.where(east_edge, sides[1], pltpu.roll(potential, cols - 1, 1))
     west = jnp.where(west_edge, sides[0], pltpu.roll(potential, 1, 1))
-    zonal = (east - west) * 0.5
     tall = north - south
-    meridional = tall * 0.5
-
-    for c in range(blocks):
-        lanes = slice(c * TILE, (c + 1) * TILE)
-        for f in range(FIELDS):
-            value = (
-                pq_ref[0, f, :, lanes].astype(jnp.float32)
-                + zonal[:, lanes] * pq_ref[1, f, :, lanes].astype(jnp.float32)
-                + meridional[:, lanes] * pq_ref[2, f, :, lanes].astype(jnp.float32)
-            )
-            moved_ref[c, f * rows : (f + 1) * rows, :] = value
-    pack_tiles(ids_ref, occ_ref, moved_ref, send_ref, rows, blocks)
+    zonal_ref[...] = (east - west) * 0.5
+    meridional_ref[...] = tall * 0.5
+
+    for r in range(rows):
+        for c in range(blocks):
+            lanes = slice(c * TILE, (c + 1) * TILE)
+            start = (r * blocks + c) * FIELDS
+            place = slice(start, start + FIELDS)
+            zonal = jnp.broadcast_to(zonal_ref[r : r + 1, lanes], (FIELDS, TILE))
+            meridional = jnp.broadcast_to(meridional_ref[r : r + 1, lanes], (FIELDS, TILE))
+            moved_ref[place, :] = (
+                still_ref[place, :]
+                + zonal * lon_ref[place, :]
+                + meridional * lat_ref[place, :]
+            )
+    pack_tiles(ids_ref, occ_ref, moved_ref, send_ref)
 
     small_row = lax.broadcasted_iota(jnp.int32, (rows, TILE), 0)
 
@@ -277,48 +371,68 @@
     weights = blocks_w[0, 0]
     smem = pl.BlockSpec(memory_space=SMEM)
     vmem = pl.BlockSpec(memory_space=VMEM)
-    hbm = pl.BlockSpec(memory_space=pl.ANY)
+    hbm = pl.BlockSpec(memory_space=pltpu.MemorySpace.HBM)
     f32 = jnp.float32
     grid = jax.ShapeDtypeStruct((rows, cols), f32)
-    moved_shape = jax.ShapeDtypeStruct((cols // TILE, FIELDS * rows, TILE), f32)
-    send_shape = jax.ShapeDtypeStruct((n_lon, CAP, FIELDS, TILE), jnp.bfloat16)
+    tile_rows = FIELDS * rows * cols // TILE
+    moved_shape = jax.ShapeDtypeStruct((tile_rows, TILE), f32)
+    send_shape = jax.ShapeDtypeStruct((n_lon * CAP * FIELDS, TILE), jnp.bfloat16)
     pay_shape = jax.ShapeDtypeStruct((n_dev, 1, 2 * cols + TILE), f32)
-    params = pltpu.CompilerParams(vmem_limit_bytes=48 << 20)
-
-    moved, send = pl.pallas_call(
-        first_kernel,
-        out_shape=(moved_shape, send_shape),
-        grid=(1,),
-        in_specs=[
-            smem,
-            smem,
-            pl.BlockSpec((pl.Squeezed(), FIELDS, rows, cols), lambda i: (0, 0, 0, 0)),
+    params = pltpu.CompilerParams(vmem_limit_bytes=5 << 20)
+
+    def in_hbm(array):
+        return pltpu.with_memory_space_constraint(array, pltpu.MemorySpace.HBM)
+
+    def in_vmem(shape):
+        return VMEM(shape.shape, shape.dtype)
+
+    early = n_lon // 2
+    block = (CAP, TILE, TILE)
+    early_shape = jax.ShapeDtypeStruct((early,) + block, weights.dtype)
+    late_shape = jax.ShapeDtypeStruct((n_lon - early,) + block, weights.dtype)
+    send, still, lon_part, lat_part, targets, coef, w_early = pl.pallas_call(
+        functools.partial(first_kernel, early),
+        out_shape=(send_shape,)
+        + (moved_shape,) * 3
+        + (
+            jax.ShapeDtypeStruct(targets.shape, targets.dtype),
+            jax.ShapeDtypeStruct(coef.shape, coef.dtype),
+            in_vmem(early_shape),
+        ),
+        in_specs=[hbm] * 6,
+        out_specs=(vmem,) * 7,
+        scratch_shapes=[
+            pltpu.SMEM(ids.shape, jnp.int32),
+            pltpu.SMEM(occ.shape, jnp.int32),
+            pltpu.VMEM(pq.shape, pq.dtype),
+            pltpu.SemaphoreType.DMA((8,)),
         ],
-        out_specs=(
-            pl.BlockSpec(moved_shape.shape, lambda i: (0, 0, 0)),
-            pl.BlockSpec(send_shape.shape, lambda i: (0, 0, 0, 0)),
-        ),
         compiler_params=params,
         name="first",
-    )(ids, occ, pq)
-
-    def interp(send, moved, det):
-        got = lax.all_to_all(send, "lon", 0, 0, tiled=True)
-        args = [targets, coef, got, weights, moved]
-        specs = [smem, smem, vmem, hbm, vmem]
-        if det is not None:
-            args.append(det)
-            specs.append(vmem)
+    )(*[in_hbm(x) for x in (ids, occ, targets, coef, pq, weights)])
+    tiles = (still, lon_part, lat_part)
+    moved = still
+    w_late = None
+
+    def interp(send, moved, det, w_late):
+        got = lax.all_to_all(send.reshape(n_lon, -1, TILE), "lon", 0, 0, tiled=True)
+        start_sweep = det is None
+        args = [targets, coef, got.reshape(send.shape), w_early]
+        out_shape = [grid, grid, pay_shape]
+        scratch = [pltpu.VMEM((tile_rows, TILE), f32)]
+        if start_sweep:
+            args += [in_hbm(weights), moved]
+            out_shape.append(in_vmem(late_shape))
+            scratch.append(pltpu.SemaphoreType.DMA((n_lon - early,)))
+        else:
+            args += [w_late, moved, det]
         return pl.pallas_call(
-            functools.partial(interp_kernel, n_lat, n_lon, det is not None),
-            out_shape=(grid, grid, pay_shape),
-            in_specs=specs,
-            out_specs=(vmem, vmem, vmem),
-            scratch_shapes=[
-                pltpu.VMEM((n_lon, CAP, TILE, TILE), jnp.bfloat16),
-                pltpu.VMEM((FIELDS * rows * cols // TILE, TILE), f32),
-                pltpu.SemaphoreType.DMA((n_lon,)),
-            ],
+            functools.partial(interp_kernel, n_lat, n_lon, early, start_sweep),
+            out_shape=tuple(out_shape),
+            in_specs=[smem, smem, vmem, vmem, hbm if start_sweep else vmem]
+            + [vmem] * (len(args) - 5),
+            out_specs=(vmem,) * len(out_shape),
+            scratch_shapes=scratch,
             compiler_params=params,
             name="interp",
         )(*args)
@@ -329,7 +443,8 @@
     gots = []
     potential = det = None
     for sweep in range(SWEEPS):
-        monitor, balance, pay = interp(send, moved, det)
+        monitor, balance, pay, *late = interp(send, moved, det, w_late)
+        w_late = late[0] if late else w_late
         if sweep == SWEEPS - 1:
             break
         gots.append(share(pay))
@@ -337,11 +452,12 @@
         potential, det, moved, send = pl.pallas_call(
             functools.partial(update_kernel, n_lat, n_lon, len(gots)),
             out_shape=(grid, grid, moved_shape, send_shape),
-            in_specs=[smem, smem] + [vmem] * (len(gots) + len(olds) + 3),
+            in_specs=[smem, smem] + [vmem] * (len(gots) + len(olds) + 5),
             out_specs=(vmem,) * 4,
+            scratch_shapes=[pltpu.VMEM((rows, cols), f32)] * 2,
             compiler_params=params,
             name="update",
-        )(ids, occ, *gots, *olds, monitor, balance, pq)
+        )(ids, occ, *gots, *olds, monitor, balance, *tiles)
 
     got = share(pay[:, :, 2 * cols :])
     return pl.pallas_call(

time: 119 us -> 107 us (0.90)
  Pallas kernels: 26.2 us -> 18.4 us
  local copies, waits for them, and re-layouts: 4.12 us -> 0.02 us
    pallas_call x4, Pallas kernels: 19.8 us -> 13.1 us  [the longest x3 10.3 us: interp(): pl.pallas_call(functools.partial(interp_kernel, n_lat, n_lon, early, star...]
    unnamed x20 -> x4, local copies, waits for them, and re-layouts: 4.11 us -> 0.01 us
where the time goes in v2:
time: 107 us
  blocking collectives  88 us (82%)
  Pallas kernels  18.4 us (17%)
    all_to_all x3, blocking collectives, interp(): got = lax.all_to_all(send.reshape(n_lon, -1, TILE), 'lon', 0, 0, tiled=True)  57 us
    all_to_all x3, blocking collectives, share(): return lax.all_to_all(pay, ('lat', 'lon'), 0, 0, tiled=True)  31 us
    pallas_call x3, Pallas kernels, interp(): pl.pallas_call(functools.partial(interp_kernel, n_lat, n_lon, early, star...  10.3 us
    pallas_call x2, Pallas kernels, per_device(): pl.pallas_call(functools.partial(update_kernel, n_lat, n_lon, len(gots)),...  4.34 us
    pallas_call x1, Pallas kernels, per_device(): pl.pallas_call(functools.partial(first_kernel, early), out_shape=(send_sh...  2.79 us

profile of v2, /device:TPU:0, one launch (start us, length us, event | category | flops | bytes accessed | tf_op | source)
XLA Modules:
  0.0 107.1 jit_solution(6411001687598363820)
XLA Ops:
  0.6 2.8 %first.1 = (bf16[2048,128]{1,0:T(8,128)(2,1)S(1)}, f32[2048,128]{1,0:T(8,128)S(1)}, f32[2048,128]{1,0:T(8,128)S(1)}, f32[2048,128]{1,0:T(8,128)S(1)}, s32[8,32]{...) custom-call(s32[8,32]{1,0:T(8,128)} %bitcast.16, s32[8]{0:T(128)} %bitcast.19, s32[8,32]{1,0:T(8,128)} %bitcast.24, ...), custom_call_target="tpu_custom_call" | custom-call | tf_op jit(solution)/shard_map/first/pallas_call | solution.py:393
  3.4 21.5 %all_to_all.30 = bf16[8,256,128]{2,1,0:T(8,128)(2,1)S(1)} all-to-all(bf16[8,256,128]{2,1,0:T(8,128)(2,1)S(1)} %bitcast.14), channel_id=1, replica_groups=mesh['lat'=4,'lon'=8] {'lon'}, dimensions={0} | all-to-all | bytes 1048576 | tf_op jit(solution)/shard_map/all_to_all | solution.py:418
  24.9 0.0 copy-start
  24.9 0.0 copy-start.1
  24.9 3.6 %interp.3 = (f32[64,512]{1,0:T(8,128)S(1)}, f32[64,512]{1,0:T(8,128)S(1)}, f32[32,1,1152]{2,1,0:T(1,128)S(1)}, bf16[4,32,128,128]{3,2,1,0:T(8,128)(2,1)S(1)}) custom-call(s32[8,32]{1,0:T(8,128)S(1)} %get-tuple-element.27.refs_0_, f32[8]{0:T(128)S(1)} %get-tuple-element.28.refs_1_, bf16[2048,128]{1,0:T(8,128)(2,1)S(1)} %bitcast.12, ...), custom_call_target="tpu_custom_call" | custom-call | tf_op jit(solution)/shard_map/interp/pallas_call | solution.py:429
  28.5 11.7 %all_to_all.31.refs_2_ = f32[32,1,1152]{2,1,0:T(1,128)S(1)} all-to-all(f32[32,1,1152]{2,1,0:T(1,128)S(1)} %get-tuple-element.32), channel_id=1, replica_groups=mesh['lat'=4,'lon'=8] {'lat','lon'}, dimensions={0} | all-to-all | bytes 294912 | tf_op jit(solution)/shard_map/all_to_all | solution.py:441
  40.2 0.0 copy-done
  40.2 0.0 copy-done.1
  40.2 2.1 %update.2 = (f32[64,512]{1,0:T(8,128)S(1)}, f32[64,512]{1,0:T(8,128)S(1)}, f32[2048,128]{1,0:T(8,128)S(1)}, bf16[2048,128]{1,0:T(8,128)(2,1)S(1)}) custom-call(s32[8,32]{1,0:T(8,128)S(1)} %bitcast.17, s32[8]{0:T(128)S(1)} %bitcast.20, f32[32,1,1152]{2,1,0:T(1,128)S(1)} %all_to_all.31.refs_2_, f32[64,512]{1,0:T(8,128)S(1)} %get-tuple-element.33.refs_3_, ...), custom_call_target="tpu_custom_call" | custom-call | tf_op jit(solution)/shard_map/update/pallas_call | solution.py:452
  42.3 17.7 %all_to_all.32 = bf16[8,256,128]{2,1,0:T(8,128)(2,1)S(1)} all-to-all(bf16[8,256,128]{2,1,0:T(8,128)(2,1)S(1)} %bitcast.15), channel_id=1, replica_groups=mesh['lat'=4,'lon'=8] {'lon'}, dimensions={0} | all-to-all | bytes 1048576 | tf_op jit(solution)/shard_map/all_to_all | solution.py:418
  60.1 3.4 %interp.4 = (f32[64,512]{1,0:T(8,128)S(1)}, f32[64,512]{1,0:T(8,128)S(1)}, f32[32,1,1152]{2,1,0:T(1,128)S(1)}) custom-call(s32[8,32]{1,0:T(8,128)S(1)} %get-tuple-element.27.refs_0_, f32[8]{0:T(128)S(1)} %get-tuple-element.28.refs_1_, bf16[2048,128]{1,0:T(8,128)(2,1)S(1)} %bitcast.11, bf16[4,32,128,128]{3,2,1,0:T(8,128)(2,1)S(1)} %get-tuple-element.30.refs_3_, ...), custom_call_target="tpu_custom_call" | custom-call | tf_op jit(solution)/shard_map/interp/pallas_call | solution.py:429
  63.5 10.2 %all_to_all.33.refs_3_ = f32[32,1,1152]{2,1,0:T(1,128)S(1)} all-to-all(f32[32,1,1152]{2,1,0:T(1,128)S(1)} %get-tuple-element.41), channel_id=1, replica_groups=mesh['lat'=4,'lon'=8] {'lat','lon'}, dimensions={0} | all-to-all | bytes 294912 | tf_op jit(solution)/shard_map/all_to_all | solution.py:441
  73.7 2.2 %update.3 = (f32[64,512]{1,0:T(8,128)S(1)}, f32[64,512]{1,0:T(8,128)S(1)}, f32[2048,128]{1,0:T(8,128)S(1)}, bf16[2048,128]{1,0:T(8,128)(2,1)S(1)}) custom-call(s32[8,32]{1,0:T(8,128)S(1)} %bitcast.18, s32[8]{0:T(128)S(1)} %bitcast.21, f32[32,1,1152]{2,1,0:T(1,128)S(1)} %all_to_all.31.refs_2_, f32[32,1,1152]{2,1,0:T(1,128)S(1)} %all_to_all.33.refs_3_, ...), custom_call_target="tpu_custom_call" | custom-call | tf_op jit(solution)/shard_map/update/pallas_call | solution.py:452
  75.9 17.7 %all_to_all.34 = bf16[8,256,128]{2,1,0:T(8,128)(2,1)S(1)} all-to-all(bf16[8,256,128]{2,1,0:T(8,128)(2,1)S(1)} %bitcast.13), channel_id=1, replica_groups=mesh['lat'=4,'lon'=8] {'lon'}, dimensions={0} | all-to-all | bytes 1048576 | tf_op jit(solution)/shard_map/all_to_all | solution.py:418
  93.7 3.4 %interp.5 = (f32[64,512]{1,0:T(8,128)S(1)}, f32[64,512]{1,0:T(8,128)S(1)}, f32[32,1,1152]{2,1,0:T(1,128)S(1)}) custom-call(s32[8,32]{1,0:T(8,128)S(1)} %get-tuple-element.27.refs_0_, f32[8]{0:T(128)S(1)} %get-tuple-element.28.refs_1_, bf16[2048,128]{1,0:T(8,128)(2,1)S(1)} %bitcast.10, bf16[4,32,128,128]{3,2,1,0:T(8,128)(2,1)S(1)} %get-tuple-element.30.refs_3_, ...), custom_call_target="tpu_custom_call" | custom-call | tf_op jit(solution)/shard_map/interp/pallas_call | solution.py:429
  97.0 9.1 %all_to_all.35.got_ref = f32[32,1,128]{2,1,0:T(1,128)S(1)} all-to-all(f32[32,1,128]{2,1,0:T(1,128)S(1)} %slice.3), channel_id=1, replica_groups=mesh['lat'=4,'lon'=8] {'lat','lon'}, dimensions={0} | all-to-all | bytes 32768 | tf_op jit(solution)/shard_map/all_to_all | solution.py:441
  106.1 0.9 last.1
  (1 shorter events, 0.0 us)
Async XLA Ops:
  24.9 15.3 %copy-start = (s32[1,1,8,32]{3,2,1,0:T(8,128)S(1)}, s32[1,1,8,32]{3,2,1,0:T(8,128)}, u32[]{:S(2)}) copy-start(s32[1,1,8,32]{3,2,1,0:T(8,128)} %param.8) | copy-start | bytes 3076
  24.9 15.3 %copy-start.1 = (s32[1,1,8]{2,1,0:T(1,128)S(1)}, s32[1,1,8]{2,1,0:T(1,128)}, u32[]{:S(2)}) copy-start(s32[1,1,8]{2,1,0:T(1,128)} %param.9) | copy-start | bytes 100
